TPU v7x, 128 devices: a whole 4x4x4 slice. The times are simulated.
128 devices in a mesh: gr: 16 (over y_hi, z, core), gc: 8 (over x, y_lo).
Axes of the slice: x: 4, y: 4 (y_hi: 2, y_lo: 2; y = y_hi * 2 + y_lo), z: 4, core: 2. Of those that a mesh axis runs over, the one named last changes fastest.
Arguments:
- shards: bfloat16 [16, 8, 56, 18432], P('gr', 'gc'), may hold values from -4.5 to 4.5, as said below
- counts: int32 [8, 16], replicated, may hold values from 1 to 56, 448 in all within a row
Outputs:
- next_shards: float32 [16, 8, 56, 18432], P('gr', 'gc')
Inputs may be any that keep to these rules, and one draw needn't show every extreme that they name: Each row of counts sums to 448: the devices (0, c) to (15, c) together hold row block c of the iterate, in order of g. `shards`: rows of a buffer at or beyond its device's count are not part of the iterate and hold arbitrary values.
All inputs are finite; a program needn't handle non-finite values.
Results may differ from a plain program's by a relative error of at most 0.0003.
Values may be sent and summed in bfloat16 or wider, within the bound.
A program may use at most 128 MiB of HBM per device.

v0:
```python
import jax
import jax.numpy as jnp
from jax import lax
from jax.sharding import PartitionSpec as P

M = 3584
N = 18432


linear_coef = 3.4445
cubic_coef = -4.775
quintic_coef = 2.0315
highest = lax.Precision.HIGHEST


def rows_against(left_rows, right_rows):
    return lax.dot_general(
        left_rows, right_rows, (((1,), (1,)), ((), ())), preferred_element_type=jnp.float32
    )


def make_accumulate(panel, sub_width, running, segment):
    seg_width = segment.shape[1]

    def one_turn(turn_index, summed):
        seg_part = lax.dynamic_slice_in_dim(segment, turn_index * sub_width, sub_width, 1)
        panel_rows = lax.dynamic_slice_in_dim(panel, turn_index * sub_width, sub_width, 0).astype(
            jnp.float32
        )
        return summed + jnp.dot(
            seg_part, panel_rows, precision=highest, preferred_element_type=jnp.float32
        )

    return lax.fori_loop(0, seg_width // sub_width, one_turn, running)


def body(shards, counts):
    own_rows = shards[0, 0]
    grid_rows = lax.axis_size("gr")
    grid_cols = lax.axis_size("gc")
    row_block = lax.axis_index("gc")
    capacity = own_rows.shape[0]
    full_width = own_rows.shape[1]
    col_width = full_width // grid_rows
    block_rows = M // grid_cols
    gram_width = M // grid_rows
    my_counts = lax.dynamic_index_in_dim(counts, row_block, 0, keepdims=False)
    my_starts = jnp.cumsum(my_counts) - my_counts
    received = lax.all_to_all(own_rows, "gr", split_axis=1, concat_axis=0, tiled=True)
    position = jnp.arange(block_rows, dtype=jnp.int32)
    holder = jnp.sum((my_starts[None, :] <= position[:, None]).astype(jnp.int32), axis=1) - 1
    one_hot = holder[:, None] == jnp.arange(grid_rows, dtype=jnp.int32)[None, :]
    first_row = jnp.sum(jnp.where(one_hot, my_starts[None, :], 0), axis=1)
    source_rows = holder * capacity + position - first_row
    own_block = jnp.take(received, source_rows, axis=0)
    panel = lax.all_gather(own_block, "gc", axis=0, tiled=True)
    partial_value = rows_against(own_block, panel)
    gram_block = lax.psum_scatter(partial_value, "gr", scatter_dimension=1, tiled=True) / N
    gram_cols = lax.all_gather(gram_block, "gc", axis=0, tiled=True)
    square_part = lax.dot_general(
        gram_block,
        gram_cols,
        (((1,), (1,)), ((), ())),
        precision=highest,
        preferred_element_type=jnp.float32,
    )
    square_block = lax.psum_scatter(square_part, "gr", scatter_dimension=1, tiled=True)
    poly_block = cubic_coef * gram_block + quintic_coef * square_block
    start_sum = jnp.zeros((block_rows, col_width), jnp.float32)
    product = make_accumulate(
        panel, gram_width, start_sum, lax.all_gather(poly_block, "gr", axis=1, tiled=True)
    )
    update_block = linear_coef * own_block.astype(jnp.float32) + product
    slot_ids = jnp.arange(capacity, dtype=jnp.int32)
    target_rows = jnp.minimum(my_starts[:, None] + slot_ids[None, :], block_rows - 1).reshape(-1)
    is_live = (slot_ids[None, :] < my_counts[:, None]).reshape(-1)
    outgoing = jnp.where(
        is_live[:, None], jnp.take(update_block, target_rows, axis=0), jnp.zeros((), jnp.float32)
    )
    returned = lax.all_to_all(outgoing, "gr", split_axis=0, concat_axis=1, tiled=True)
    return returned.reshape(1, 1, capacity, full_width)


def solution(mesh):
    placed = (P("gr", "gc", None, None), P())
    return jax.shard_map(
        body, mesh=mesh, in_specs=placed, out_specs=P("gr", "gc", None, None), check_vma=False
    )
```

profile of v0, /device:TPU:1, one launch (start us, length us, event | category | flops | bytes accessed | tf_op | source)
XLA Modules:
  0.0 709.8 jit_solution(17190910258514315236)
XLA Ops:
  10.1 9.5 %all-to-all-start = ((bf16[56,16,1152]{2,0,1:T(8,128)(2,1)}), bf16[56,16,1152]{2,0,1:T(8,128)(2,1)S(1)}, u32[]{:S(2)}, u32[]{:S(2)}) async-start(bf16[56,16,1152]{2,0,1:T(8,128)(2,1)} %copy.15), calls=%async_computation | async-start | bytes 4128768 | tf_op jit(solution)/shard_map/all_to_all | solution.py:49
  20.1 27.6 %all-to-all-done = bf16[56,16,1152]{2,0,1:T(8,128)(2,1)S(1)} async-done(((bf16[56,16,1152]{2,0,1:T(8,128)(2,1)}), bf16[56,16,1152]{2,0,1:T(8,128)(2,1)S(1)}, u32[]{:S(2)}, u32[]{:S(2)}) %all-to-all-start) | async-done | bytes 2064416 | tf_op jit(solution)/shard_map/all_to_all | solution.py:49
  47.6 2.3 gather_fusion
  51.2 166.8 %all-gather.4.cloned.1.call-done = bf16[3584,1152]{1,0:T(8,128)(2,1)} async-done(((bf16[448,1152]{1,0:T(8,128)(2,1)}), bf16[3584,1152]{1,0:T(8,128)(2,1)}) %all-gather.4.cloned.1.call-update) | async-done | bytes 8257552 | tf_op jit(solution)/shard_map/all_gather | solution.py:56
  218.0 11.7 %convolution_bitcast_fusion.1 = f32[3584,448]{1,0:T(8,128)} fusion(bf16[448,1152]{1,0:T(8,128)(2,1)} %broadcast_select_fusion, bf16[3584,1152]{1,0:T(8,128)(2,1)} %all-gather.4.cloned.1.call-done), kind=kOutput, calls=%fused_computation.7 | convolution fusion | flops 3699376128 | bytes 15712256
  229.7 98.5 %reduce-scatter.7.cloned.1.call-done = f32[224,448]{1,0:T(8,128)} async-done(((f32[3584,448]{1,0:T(8,128)}), f32[224,448]{1,0:T(8,128)}) %reduce-scatter.7.cloned.1.call-update) | async-done | bytes 401424
  330.4 79.9 %all-gather.6.cloned.1.call-done = f32[3584,224]{1,0:T(8,128)} async-done(((f32[448,224]{1,0:T(8,128)}), f32[3584,224]{1,0:T(8,128)}) %all-gather.6.cloned.1.call-update) | async-done | bytes 3211280 | tf_op jit(solution)/shard_map/all_gather | solution.py:59
  410.3 10.0 %convolution_bitcast_fusion = f32[3584,448]{1,0:T(8,128)} fusion(f32[3584,224]{1,0:T(8,128)} %all-gather.6.cloned.1.call-done, f32[448,224]{1,0:T(8,128)S(1)} %copy.20), kind=kOutput, calls=%fused_computation.6 | convolution fusion | flops 4316039168 | bytes 10035200
  420.6 94.1 %reduce-scatter.9.cloned.1.call-done = f32[224,448]{1,0:T(8,128)} async-done(((f32[3584,448]{1,0:T(8,128)}), f32[224,448]{1,0:T(8,128)}) %reduce-scatter.9.cloned.1.call-update) | async-done | bytes 401424
  517.3 69.1 %all-gather.8.cloned.1.call-done = f32[448,3584]{0,1:T(8,128)} async-done(((f32[448,224]{0,1:T(8,128)}), f32[448,3584]{0,1:T(8,128)}) %all-gather.8.cloned.1.call-update) | async-done | bytes 6422544 | tf_op jit(solution)/shard_map/all_gather | solution.py:71
  586.3 46.5 %while.14 = (s32[]{:T(128)}, f32[448,1152]{1,0:T(8,128)S(1)}, f32[448,3584]{0,1:T(8,128)}, bf16[3584,1152]{1,0:T(8,128)(2,1)}, s32[]{:T(128)}, /*index=5*/s32[]{:T(128)}, s32[]{:T(128)}, s32[]{:T(128)}) while((s32[]{:T(128)}, f32[448,1152]{1,0:T(8,128)S(1)}, f32[448,3584]{0,1:T(8,128)}, bf16[3584,1152]{1,0:T(8,128)(2,1)}, ...), condition=%wide.region_6.7_spmd.clone, body=%wide.region_5.6_spmd.clone.sunk | while | flops 1388298240 | bytes 5105292 | solution.py:34
  586.3 2.9 convolution_add_fusion.2
  589.2 2.9 convolution_add_fusion.2
  592.1 2.9 convolution_add_fusion.2
  595.0 2.9 convolution_add_fusion.2
  597.9 2.9 convolution_add_fusion.2
  600.8 2.9 convolution_add_fusion.2
  603.8 2.9 convolution_add_fusion.2
  606.7 2.9 convolution_add_fusion.2
  609.6 2.9 convolution_add_fusion.2
  612.5 2.9 convolution_add_fusion.2
  615.4 2.9 convolution_add_fusion.2
  618.3 2.9 convolution_add_fusion.2
  621.2 2.9 convolution_add_fusion.2
  624.1 2.9 convolution_add_fusion.2
  627.0 2.9 convolution_add_fusion.2
  629.9 2.9 convolution_add_fusion.2
  636.0 4.3 gather_fusion.1
  640.4 2.5 select_select_fusion
  642.9 52.7 %all_to_all.32 = f32[16,56,1152]{2,1,0:T(8,128)S(1)} all-to-all(f32[16,56,1152]{2,1,0:T(8,128)S(1)} %select_select_fusion), channel_id=1, replica_groups=mesh['gr'=16,'gc'=8] {'gr'}, dimensions={0} | all-to-all | bytes 8257536 | tf_op jit(solution)/shard_map/all_to_all | solution.py:80
  695.6 2.7 copy.18
  698.2 5.0 reshape.143
  (42 shorter events, 13.3 us)
Async XLA Ops:
  8.4 11.2 %copy-start.1 = (s32[8,16]{1,0:T(8,128)S(1)}, s32[8,16]{1,0:T(8,128)}, u32[]{:S(2)}) copy-start(s32[8,16]{1,0:T(8,128)} %param.5) | copy-start | bytes 1540
  10.1 37.6 %all-to-all-start = ((bf16[56,16,1152]{2,0,1:T(8,128)(2,1)}), bf16[56,16,1152]{2,0,1:T(8,128)(2,1)S(1)}, u32[]{:S(2)}, u32[]{:S(2)}) async-start(bf16[56,16,1152]{2,0,1:T(8,128)(2,1)} %copy.15), calls=%async_computation | async-start | bytes 4128768 | tf_op jit(solution)/shard_map/all_to_all | solution.py:49
  19.5 198.5 %all-gather.4.cloned.1.call-start = ((), (), s32[]{:S(2)}) async-start(), calls=%async_computation.4 | async-start | bytes 9289728 | tf_op jit(solution)/shard_map/all_gather | solution.py:56
  51.1 277.1 %reduce-scatter.7.cloned.1.call-start = ((), (), s32[]{:S(2)}) async-start(), calls=%async_computation.7 | async-start | bytes 7798784
  229.7 180.6 %all-gather.6.cloned.1.call-start = ((), (), s32[]{:S(2)}) async-start(), calls=%async_computation.5 | async-start | bytes 4128768 | tf_op jit(solution)/shard_map/all_gather | solution.py:59
  330.3 184.4 %reduce-scatter.9.cloned.1.call-start = ((), (), s32[]{:S(2)}) async-start(), calls=%async_computation.8 | async-start | bytes 7798784
  420.3 166.0 %all-gather.8.cloned.1.call-start = ((), (), s32[]{:S(2)}) async-start(), calls=%async_computation.6 | async-start | bytes 7798784 | tf_op jit(solution)/shard_map/all_gather | solution.py:71
  632.8 1.3 copy-start
Sparse Core Ops, SparseCore 0:
  51.2 166.7 all-gather.3
  229.8 98.4 reduce-scatter.6
  330.4 79.8 all-gather.5
  420.5 94.1 reduce-scatter.8
  517.1 69.2 all-gather.7
where the time goes:
time: 711 us; the launch traced here: 710 us
  waiting for transfers between devices  536 us (75%)
  matrix products  67.7 us (10%)
  blocking collectives  52.7 us (7%)
  local copies, waits for them, and re-layouts  22.7 us (3%)
  between operations  13.3 us (2%)
  starting transfers between devices  9.85 us (1%)
    unnamed x7, waiting for transfers between devices  193 us
    all_gather x1, waiting for transfers between devices, body(): panel = lax.all_gather(own_block, 'gc', axis=0, tiled=True)  167 us
    all_gather x1, waiting for transfers between devices, body(): gram_cols = lax.all_gather(gram_block, 'gc', axis=0, tiled=True)  79.9 us
    all_gather x1, waiting for transfers between devices, body(): lax.all_gather(poly_block, 'gr', axis=1, tiled=True)  69.1 us
    all_to_all x1, blocking collectives, body(): lax.all_to_all(outgoing, 'gr', split_axis=0, concat_axis=1, tiled=True)  52.7 us
    dot_general x16, matrix products, one_turn(): jnp.dot(seg_part, panel_rows, precision=highest, preferred_element_type=j...  46 us
    all_to_all x1, waiting for transfers between devices, body(): lax.all_to_all(own_rows, 'gr', split_axis=1, concat_axis=0, tiled=True)  27.6 us
    unnamed x2, matrix products  21.7 us
  transfers between devices with their start and end apart: 6, of which 6 were waited for; matrix products, arithmetic and copies ran while one was open for 0% of the time, Pallas kernels for 0%

commit v1 on v0

v1 whole, which is shorter than its diff:
```python
import jax
import jax.numpy as jnp
from jax import lax
from jax.experimental import pallas as pl
from jax.experimental.pallas import tpu as pltpu
from jax.sharding import PartitionSpec as P

M = 3584
N = 18432
CAP = 56
RB = 448
WIDTH = 1152
PIECE_ROWS = 112
PIECE_COLS = 896

linear_coef = 3.4445
cubic_coef = -4.775
quintic_coef = 2.0315

MESH = pl.DeviceIdType.MESH
f32 = jnp.float32
bf16 = jnp.bfloat16


def mod(value, size):
    return lax.rem(value, jnp.int32(size))


def position():
    gr = lax.axis_index("gr")
    gc = lax.axis_index("gc")
    half = lax.div(gr, jnp.int32(2))
    x = lax.div(gc, jnp.int32(2))
    y = lax.div(half, jnp.int32(4)) * 2 + mod(gc, 2)
    return x, y, mod(half, 4), mod(gr, 2)


def device(x, y, z, core):
    return {
        "gr": (lax.div(y, jnp.int32(2)) * 4 + z) * 2 + core,
        "gc": x * 2 + mod(y, 2),
    }


def greet(x, y, z, core):
    barrier = pltpu.get_barrier_semaphore()
    count = 0
    for dy in range(4):
        for dz in range(4):
            for dc in range(2):
                if dy or dz or dc:
                    target = device(x, mod(y + dy, 4), mod(z + dz, 4), mod(core + dc, 2))
                    pl.semaphore_signal(barrier, inc=1, device_id=target, device_id_type=MESH)
                    count += 1
    for dx in (1, 3):
        target = device(mod(x + dx, 4), y, z, core)
        pl.semaphore_signal(barrier, inc=1, device_id=target, device_id_type=MESH)
        count += 1
    pl.semaphore_wait(barrier, count)


class Courier:
    def __init__(self, send_sem, recv_sem):
        self.send_sem, self.recv_sem = send_sem, recv_sem
        self.copies = []

    def send(self, src, dst, target):
        index = len(self.copies)
        copy = pltpu.make_async_remote_copy(
            src_ref=src,
            dst_ref=dst,
            send_sem=self.send_sem.at[index],
            recv_sem=self.recv_sem.at[index],
            device_id=target,
            device_id_type=MESH,
        )
        self.copies.append(copy)
        copy.start()
        return copy

    def drain(self):
        for copy in self.copies:
            copy.wait_send()


class RingGather:
    def __init__(self, courier, part_a, part_b, pos, right, left):
        self.courier, self.part_a, self.part_b = courier, part_a, part_b
        self.pos, self.right, self.left = pos, right, left
        a, b = part_a(pos), part_b(pos)
        self.a_right = courier.send(a, a, right)
        self.b_left = courier.send(b, b, left)
        self.b_right = courier.send(b, b, right)
        self.a_left = courier.send(a, a, left)

    def relay(self):
        self.a_right.wait_recv()
        a = self.part_a(mod(self.pos + 3, 4))
        self.a_far = self.courier.send(a, a, self.right)
        self.b_left.wait_recv()
        b = self.part_b(mod(self.pos + 1, 4))
        self.b_far = self.courier.send(b, b, self.left)

    def near(self):
        self.b_right.wait_recv()
        self.a_left.wait_recv()

    def far(self):
        self.a_far.wait_recv()
        self.b_far.wait_recv()


class RingReduce:
    def __init__(self, courier, part_a, part_b, bufs, cut, pos, right, left):
        self.courier, self.part_a, self.part_b = courier, part_a, part_b
        self.pos, self.right, self.left = pos, right, left
        self.tmp_a, self.tmp_b, self.from_left, self.from_right = bufs
        self.in_a, self.in_b = cut
        far = mod(pos + 2, 4)
        self.a1 = courier.send(part_a(far), self.tmp_a, right)
        self.b1 = courier.send(part_b(far), self.tmp_b, left)
        self.a2 = courier.send(part_b(mod(pos + 1, 4)), self.in_b(self.from_left), right)
        self.b2 = courier.send(part_a(mod(pos + 3, 4)), self.in_a(self.from_right), left)

    def relay(self):
        self.a1.wait_recv()
        a = self.part_a(mod(self.pos + 1, 4))
        a[...] = a[...] + self.tmp_a[...]
        self.a3 = self.courier.send(a, self.in_a(self.from_left), self.right)
        self.b1.wait_recv()
        b = self.part_b(mod(self.pos + 3, 4))
        b[...] = b[...] + self.tmp_b[...]
        self.b3 = self.courier.send(b, self.in_b(self.from_right), self.left)

    def finish(self):
        for copy in (self.a2, self.b2, self.a3, self.b3):
            copy.wait_recv()


def gram_kernel(
    shard, target_rows, panel, gram_piece, received, wide, part,
    big_tmp, big_recv, small_tmp_a, small_tmp_b, small_recv,
    send_sem, recv_sem, in_send, in_recv,
):
    x, y, z, core = position()
    greet(x, y, z, core)
    y_lo = mod(y, 2)
    me = lax.axis_index("gr")
    at_home = core == y_lo

    def columns(dy, dz):
        block = mod(y + dy, 4) * 4 + mod(z + dz, 4)
        return shard.at[:, pl.ds(pl.multiple_of(block * WIDTH, 128), WIDTH)]

    def outward(index, dy, dz):
        return pltpu.make_async_remote_copy(
            src_ref=columns(dy, dz),
            dst_ref=received.at[me],
            send_sem=in_send.at[index],
            recv_sem=in_recv.at[me],
            device_id=device(x, mod(y + dy, 4), mod(z + dz, 4), y_lo),
            device_id_type=MESH,
        )

    offsets = [(dy, dz) for dy in range(4) for dz in range(4)]
    offsets = sorted(offsets, key=lambda o: -(min(o[0], 4 - o[0]) + min(o[1], 4 - o[1])))
    for index, (dy, dz) in enumerate(offsets):
        if dy or dz:
            outward(index, dy, dz).start()
        else:
            @pl.when(at_home)
            def _():
                pltpu.make_async_copy(columns(0, 0), received.at[me], in_recv.at[me]).start()

            @pl.when(jnp.logical_not(at_home))
            def _():
                outward(index, 0, 0).start()
    for g in range(16):
        pltpu.make_async_copy(received.at[g], received.at[g], in_recv.at[g]).wait()
        wide[g * CAP:(g + 1) * CAP] = received[g].astype(f32)

    rows = lax.broadcasted_iota(jnp.int32, (RB, 16 * CAP), 0)
    pick = (rows == target_rows[...]).astype(f32).astype(bf16)
    own = panel.at[x, pl.ds(pl.multiple_of(core * RB, RB), RB)]
    for low, size in ((0, 512), (512, 640)):
        own[:, low:low + size] = jnp.dot(
            pick, wide[:, low:low + size].astype(bf16), preferred_element_type=f32
        ).astype(bf16)

    courier = Courier(send_sem, recv_sem)
    partner = device(x, y, z, 1 - core)

    def slot(low):
        def part_of(pos):
            return panel.at[pos, pl.ds(pl.multiple_of(core * RB + low, 32), RB // 2)]
        return part_of

    def whole(pos):
        return panel.at[pos, pl.ds(pl.multiple_of(core * RB, 32), RB)]

    ring = RingGather(
        courier, slot(0), slot(RB // 2), x,
        device(mod(x + 1, 4), y, z, core), device(mod(x + 3, 4), y, z, core),
    )
    across = [courier.send(whole(x), whole(x), partner)]

    def multiply(pos):
        product = lax.dot_general(
            own[...], panel[pos], (((1,), (1,)), ((), ())), preferred_element_type=f32
        )
        part[pos] = (product * (1.0 / N)).reshape(4, 2, CAP, PIECE_COLS)

    ring.relay()
    ring.near()
    for step in (1, 3):
        pos = mod(x + step, 4)
        across.append(courier.send(whole(pos), whole(pos), partner))
    across[0].wait_recv()
    multiply(x)
    across[1].wait_recv()
    multiply(mod(x + 1, 4))
    across[2].wait_recv()
    multiply(mod(x + 3, 4))
    ring.far()
    pos = mod(x + 2, 4)
    across.append(courier.send(whole(pos), whole(pos), partner))
    across[3].wait_recv()
    multiply(pos)

    z_right, z_left = device(x, y, mod(z + 1, 4), core), device(x, y, mod(z + 3, 4), core)
    y_right, y_left = device(x, mod(y + 1, 4), z, core), device(x, mod(y + 3, 4), z, core)
    first, second = (lambda r: r.at[0:2]), (lambda r: r.at[2:4])
    upper, lower = (lambda r: r.at[0:32]), (lambda r: r.at[32:CAP])

    def bufs(tmp_a, tmp_b, recv, half):
        return tmp_a.at[half], tmp_b.at[half], recv.at[half, 0], recv.at[half, 1]

    big = lambda half: bufs(big_tmp.at[0], big_tmp.at[1], big_recv, half)
    small = lambda half: bufs(small_tmp_a, small_tmp_b, small_recv, half)
    one = RingReduce(
        courier, lambda p: part.at[0:2, p, 0], lambda p: part.at[2:4, p, 0],
        big(0), (first, second), z, z_right, z_left,
    )
    two = RingReduce(
        courier, lambda p: part.at[p, 0:2, 1], lambda p: part.at[p, 2:4, 1],
        big(1), (first, second), y, y_right, y_left,
    )
    one.relay()
    two.relay()
    one.finish()
    part[:, z, 0] = part[:, z, 0] + big_recv[0, 0] + big_recv[0, 1]
    three = RingReduce(
        courier, lambda p: upper(part.at[p, z, 0]), lambda p: lower(part.at[p, z, 0]),
        small(0), (upper, lower), y, y_right, y_left,
    )
    two.finish()
    part[y, :, 1] = part[y, :, 1] + big_recv[1, 0] + big_recv[1, 1]
    four = RingReduce(
        courier, lambda p: upper(part.at[y, p, 1]), lambda p: lower(part.at[y, p, 1]),
        small(1), (upper, lower), z, z_right, z_left,
    )
    three.relay()
    four.relay()
    three.finish()
    gram_piece[0:CAP] = part[y, z, 0] + small_recv[0, 0] + small_recv[0, 1]
    four.finish()
    gram_piece[CAP:2 * CAP] = part[y, z, 1] + small_recv[1, 0] + small_recv[1, 1]
    courier.drain()
    for index, (dy, dz) in enumerate(offsets):
        if dy or dz:
            outward(index, dy, dz).wait_send()
        else:
            @pl.when(jnp.logical_not(at_home))
            def _():
                outward(index, 0, 0).wait_send()


def split(value):
    high = value.astype(bf16)
    return high, (value - high.astype(f32)).astype(bf16)


def update_kernel(
    slot_rows, gram_piece, panel, result, gram_cols, gram_rows, square, poly,
    pick, outgoing, send_sem, recv_sem, out_send, out_recv,
):
    x, y, z, core = position()
    greet(x, y, z, core)
    courier = Courier(send_sem, recv_sem)
    partner = device(x, y, z, 1 - core)
    z_right, z_left = device(x, y, mod(z + 1, 4), core), device(x, y, mod(z + 3, 4), core)
    y_right, y_left = device(x, mod(y + 1, 4), z, core), device(x, mod(y + 3, 4), z, core)
    x_right, x_left = device(mod(x + 1, 4), y, z, core), device(mod(x + 3, 4), y, z, core)

    for h, value in enumerate(split(gram_piece[...])):
        gram_cols[h, x, core, z] = value
        gram_rows[h, y] = value
    upper, lower = (lambda r: r.at[0:64]), (lambda r: r.at[64:PIECE_ROWS])

    def forward(ref):
        return courier.send(ref, ref, partner)

    hi_z = RingGather(
        courier, lambda p: upper(gram_cols.at[0, x, core, p]),
        lambda p: lower(gram_cols.at[0, x, core, p]), z, z_right, z_left,
    )
    lo_x = RingGather(
        courier, lambda p: upper(gram_cols.at[1, p, core, z]),
        lambda p: lower(gram_cols.at[1, p, core, z]), x, x_right, x_left,
    )
    rows_y = RingGather(
        courier, lambda p: gram_rows.at[0, p], lambda p: gram_rows.at[1, p], y, y_right, y_left,
    )
    hi_z.relay()
    lo_x.relay()
    hi_z.near()
    hi_z.far()
    hi_x = RingGather(
        courier, lambda p: gram_cols.at[0, p, core, 0:2],
        lambda p: gram_cols.at[0, p, core, 2:4], x, x_right, x_left,
    )
    across = [forward(gram_cols.at[0, x, core])]
    lo_x.near()
    lo_x.far()
    lo_z = RingGather(
        courier, lambda p: gram_cols.at[1, 0:2, core, p],
        lambda p: gram_cols.at[1, 2:4, core, p], z, z_right, z_left,
    )
    across.append(forward(gram_cols.at[1, :, core, z]))
    rows_y.relay()
    hi_x.relay()
    lo_z.relay()
    rows_y.near()
    rows_y.far()
    hi_x.near()
    for step in (1, 3):
        across.append(forward(gram_cols.at[0, mod(x + step, 4), core]))
    lo_z.near()
    for step in (1, 3):
        across.append(forward(gram_cols.at[1, :, core, mod(z + step, 4)]))
    hi_x.far()
    across.append(forward(gram_cols.at[0, mod(x + 2, 4), core]))
    lo_z.far()
    across.append(forward(gram_cols.at[1, :, core, mod(z + 2, 4)]))
    for copy in across:
        copy.wait_recv()

    square[...] = jnp.zeros_like(square)

    @pl.loop(0, 4)
    def _(m):
        high = gram_cols[0, m].reshape(PIECE_COLS, PIECE_COLS)
        low = gram_cols[1, m].reshape(PIECE_COLS, PIECE_COLS)
        left = jnp.concatenate([gram_rows[0, m], gram_rows[1, m]], axis=0)
        both = jnp.dot(left, high, preferred_element_type=f32)
        square[...] += (
            both[0:PIECE_ROWS] + both[PIECE_ROWS:]
            + jnp.dot(gram_rows[0, m], low, preferred_element_type=f32)
        )

    for h, value in enumerate(split(cubic_coef * gram_piece[...] + quintic_coef * square[...])):
        poly[h, y, z] = value
    hi_z = RingGather(
        courier, lambda p: upper(poly.at[0, y, p]), lambda p: lower(poly.at[0, y, p]),
        z, z_right, z_left,
    )
    lo_y = RingGather(
        courier, lambda p: upper(poly.at[1, p, z]), lambda p: lower(poly.at[1, p, z]),
        y, y_right, y_left,
    )
    hi_z.relay()
    lo_y.relay()
    hi_z.near()
    hi_z.far()
    hi_y = RingGather(
        courier, lambda p: poly.at[0, p, 0:2], lambda p: poly.at[0, p, 2:4], y, y_right, y_left,
    )
    lo_y.near()
    lo_y.far()
    lo_z = RingGather(
        courier, lambda p: poly.at[1, 0:2, p], lambda p: poly.at[1, 2:4, p], z, z_right, z_left,
    )
    hi_y.relay()
    lo_z.relay()
    hi_y.near()
    lo_z.near()
    hi_y.far()
    lo_z.far()

    block = y * 4 + z
    at_home = core == mod(y, 2)
    own = panel.at[x, pl.ds(pl.multiple_of(core * RB, RB), RB)]
    chunks = ((0, 512), (512, 640))
    offsets = [(dh, dz, dc) for dh in (1, 0) for dz in (2, 1, 3, 0) for dc in (1, 0)]

    def place(dh, dz, dc):
        y_to = core + 2 * mod(lax.div(y, jnp.int32(2)) + dh, 2)
        z_to, core_to = mod(z + dz, 4), mod(core + dc, 2)
        return y_to, z_to, core_to

    def window(source, low, size):
        return result.at[:, pl.ds(pl.multiple_of(source * WIDTH + low, 128), size)]

    def outward(chunk, index, offset):
        low, size = chunks[chunk]
        y_to, z_to, core_to = place(*offset)
        return pltpu.make_async_remote_copy(
            src_ref=outgoing.at[index, :, low:low + size],
            dst_ref=window(block, low, size),
            send_sem=out_send.at[chunk, index],
            recv_sem=out_recv.at[chunk, block],
            device_id=device(x, y_to, z_to, core_to),
            device_id_type=MESH,
        )

    row_ids = lax.broadcasted_iota(jnp.int32, (CAP, RB), 1)
    for index, offset in enumerate(offsets):
        y_to, z_to, core_to = place(*offset)
        g = (lax.div(y_to, jnp.int32(2)) * 4 + z_to) * 2 + core_to
        pick[index * CAP:(index + 1) * CAP] = (row_ids == slot_rows[g]).astype(f32)

    for chunk, (low, size) in enumerate(chunks):
        total = linear_coef * own[:, low:low + size].astype(f32)
        for m in range(4):
            for h in range(2):
                total = total + jnp.dot(
                    poly[h, m].reshape(RB, PIECE_COLS), panel[m, :, low:low + size],
                    preferred_element_type=f32,
                )
        high, rest = split(total)
        moved = jnp.dot(pick[...].astype(bf16), high, preferred_element_type=f32)
        moved = moved + jnp.dot(pick[...].astype(bf16), rest, preferred_element_type=f32)
        outgoing[:, :, low:low + size] = moved.reshape(16, CAP, size)
        for index, offset in enumerate(offsets):
            if any(offset):
                outward(chunk, index, offset).start()
            else:
                @pl.when(at_home)
                def _():
                    pltpu.make_async_copy(
                        outgoing.at[index, :, low:low + size], window(block, low, size),
                        out_recv.at[chunk, block],
                    ).start()

                @pl.when(jnp.logical_not(at_home))
                def _():
                    outward(chunk, index, offset).start()
    for chunk, (low, size) in enumerate(chunks):
        for source in range(16):
            pltpu.make_async_copy(
                window(source, low, size), window(source, low, size), out_recv.at[chunk, source]
            ).wait()
    courier.drain()
    for chunk in range(len(chunks)):
        for index, offset in enumerate(offsets):
            if any(offset):
                outward(chunk, index, offset).wait_send()
            else:
                @pl.when(jnp.logical_not(at_home))
                def _():
                    outward(chunk, index, offset).wait_send()


VMEM_LIMIT = 64000 * 1024
in_vmem = pl.BlockSpec(memory_space=pltpu.VMEM)
anywhere = pl.BlockSpec(memory_space=pl.ANY)


def body(shards, counts):
    x, _, _, core = position()
    row_block = x * 2 + core
    my_counts = lax.dynamic_slice_in_dim(counts, row_block, 1, 0)
    my_starts = jnp.cumsum(my_counts, axis=1) - my_counts
    slots = jnp.arange(CAP, dtype=jnp.int32)[None, :]
    target_rows = jnp.where(
        slots < my_counts[0][:, None], my_starts[0][:, None] + slots, -1
    ).reshape(1, 16 * CAP)

    panel, gram_piece = pl.pallas_call(
        gram_kernel,
        name="gram_kernel",
        out_shape=(
            jax.ShapeDtypeStruct((4, 2 * RB, WIDTH), bf16),
            jax.ShapeDtypeStruct((PIECE_ROWS, PIECE_COLS), f32),
        ),
        in_specs=[anywhere, in_vmem],
        out_specs=(in_vmem, in_vmem),
        scratch_shapes=[
            pltpu.VMEM((16, CAP, WIDTH), bf16),
            pltpu.VMEM((16 * CAP, WIDTH), f32),
            pltpu.VMEM((4, 4, 2, CAP, PIECE_COLS), f32),
            pltpu.VMEM((2, 2, 2, CAP, PIECE_COLS), f32),
            pltpu.VMEM((2, 2, 4, CAP, PIECE_COLS), f32),
            pltpu.VMEM((2, 32, PIECE_COLS), f32),
            pltpu.VMEM((2, CAP - 32, PIECE_COLS), f32),
            pltpu.VMEM((2, 2, CAP, PIECE_COLS), f32),
            pltpu.SemaphoreType.DMA((40,)),
            pltpu.SemaphoreType.DMA((40,)),
            pltpu.SemaphoreType.DMA((16,)),
            pltpu.SemaphoreType.DMA((16,)),
        ],
        compiler_params=pltpu.CompilerParams(
            collective_id=0, has_side_effects=True, vmem_limit_bytes=VMEM_LIMIT
        ),
    )(shards[0, 0], target_rows)

    result = pl.pallas_call(
        update_kernel,
        name="update_kernel",
        out_shape=jax.ShapeDtypeStruct((CAP, N), f32),
        in_specs=[in_vmem, in_vmem, in_vmem],
        out_specs=anywhere,
        scratch_shapes=[
            pltpu.VMEM((2, 4, 2, 4, PIECE_ROWS, PIECE_COLS), bf16),
            pltpu.VMEM((2, 4, PIECE_ROWS, PIECE_COLS), bf16),
            pltpu.VMEM((PIECE_ROWS, PIECE_COLS), f32),
            pltpu.VMEM((2, 4, 4, PIECE_ROWS, PIECE_COLS), bf16),
            pltpu.VMEM((16 * CAP, RB), f32),
            pltpu.VMEM((16, CAP, WIDTH), f32),
            pltpu.SemaphoreType.DMA((64,)),
            pltpu.SemaphoreType.DMA((64,)),
            pltpu.SemaphoreType.DMA((2, 16)),
            pltpu.SemaphoreType.DMA((2, 16)),
        ],
        compiler_params=pltpu.CompilerParams(
            collective_id=1, has_side_effects=True, vmem_limit_bytes=VMEM_LIMIT
        ),
    )(target_rows.reshape(16, CAP, 1), gram_piece, panel)
    return result.reshape(1, 1, CAP, N)


def solution(mesh):
    placed = (P("gr", "gc", None, None), P())
    return jax.shard_map(
        body, mesh=mesh, in_specs=placed, out_specs=P("gr", "gc", None, None), check_vma=False
    )
```

time: 711 us -> 280 us (0.39)
  waiting for transfers between devices: 536 us -> 0 us
  Pallas kernels: 0 us -> 267 us
  matrix products: 67.7 us -> 0 us
  blocking collectives: 52.7 us -> 0 us
  local copies, waits for them, and re-layouts: 22.7 us -> 6.49 us
  between operations: 13.3 us -> 0.02 us
  starting transfers between devices: 9.85 us -> 0 us
    all_gather x3 -> x0, waiting for transfers between devices: 316 us -> none  [the longest x1 167 us: body(): panel = lax.all_gather(own_block, 'gc', axis=0, tiled=True)]
    pallas_call x0 -> x2, Pallas kernels: none -> 267 us  [the longest x1 147 us: body(): pl.pallas_call(update_kernel, name='update_kernel', out_shape=jax.ShapeDt...]
    unnamed x7 -> x0, waiting for transfers between devices: 193 us -> none
    all_to_all x1 -> x0, blocking collectives: 52.7 us -> none  [body(): lax.all_to_all(outgoing, 'gr', split_axis=0, concat_axis=1, tiled=True)]
    dot_general x16 -> x0, matrix products: 46 us -> none  [one_turn(): jnp.dot(seg_part, panel_rows, precision=highest, preferred_element_type=j...]
    all_to_all x1 -> x0, waiting for transfers between devices: 27.6 us -> none  [body(): lax.all_to_all(own_rows, 'gr', split_axis=1, concat_axis=0, tiled=True)]
    unnamed x2 -> x0, matrix products: 21.7 us -> none
    all_to_all x1 -> x0, starting transfers between devices: 9.46 us -> none  [body(): lax.all_to_all(own_rows, 'gr', split_axis=1, concat_axis=0, tiled=True)]
  transfers between devices with their start and end apart: 6 -> 0, of which waited for: 6 -> 0; matrix products, arithmetic and copies ran while one was open for 0% -> 0% of each run, Pallas kernels for 0% -> 0%
where the time goes in v1:
time: 280 us; the launch traced here: 275 us
  Pallas kernels  267 us (95%)
  local copies, waits for them, and re-layouts  6.49 us (2%)
    pallas_call x1, Pallas kernels, body(): pl.pallas_call(update_kernel, name='update_kernel', out_shape=jax.ShapeDt...  147 us
    pallas_call x1, Pallas kernels, body(): pl.pallas_call(gram_kernel, name='gram_kernel', out_shape=(jax.ShapeDtype...  119 us

profile of v1, /device:TPU:1, one launch (start us, length us, event | category | flops | bytes accessed | tf_op | source)
XLA Modules:
  0.0 275.0 jit_solution(15863380810356739530)
XLA Ops:
  0.0 0.7 fusion
  0.7 0.7 constant_dynamic-slice_fusion
  1.4 0.2 reduce_window_sum.11
  1.6 0.7 subtract_bitcast_fusion
  2.3 0.1 add_select_fusion.1
  2.3 0.7 select_n.29.target_rows
  3.0 1.0 add_select_fusion.slot_rows
  4.0 119.4 %gram_kernel.1 = (bf16[4,896,1152]{2,1,0:T(8,128)(2,1)}, f32[112,896]{1,0:T(8,128)}) custom-call(bf16[56,18432]{1,0:T(8,128)(2,1)} %bitcast.7, s32[1,896]{1,0:T(1,128)} %select_n.29.target_rows), custom_call_target="tpu_custom_call" | custom-call | tf_op jit(solution)/shard_map/gram_kernel/pallas_call | solution.py:479
  123.4 147.2 %update_kernel.1 = f32[56,18432]{1,0:T(8,128)} custom-call(s32[16,56,1]{2,1,0:T(8,128)} %add_select_fusion.slot_rows, f32[112,896]{1,0:T(8,128)} %get-tuple-element.7.gram_piece, bf16[4,896,1152]{2,1,0:T(8,128)(2,1)} %get-tuple-element.8.panel), custom_call_target="tpu_custom_call" | custom-call | tf_op jit(solution)/shard_map/update_kernel/pallas_call | solution.py:507
  270.6 4.4 %copy.4 = f32[1,1,56,18432]{3,2,1,0:T(8,128)} copy(f32[1,1,56,18432]{3,2,1,0:T(8,128)} %bitcast.6) | data formatting | bytes 8257536

commit v2 on v1

--- a/solution.py
+++ b/solution.py
@@ -140,7 +140,7 @@
 def gram_kernel(
     shard, target_rows, panel, gram_piece, received, wide, part,
     big_tmp, big_recv, small_tmp_a, small_tmp_b, small_recv,
-    send_sem, recv_sem, in_send, in_recv,
+    relay, send_sem, recv_sem, in_send, in_recv, relay_send, relay_recv,
 ):
     x, y, z, core = position()
     greet(x, y, z, core)
@@ -164,8 +164,38 @@
 
     offsets = [(dy, dz) for dy in range(4) for dz in range(4)]
     offsets = sorted(offsets, key=lambda o: -(min(o[0], 4 - o[0]) + min(o[1], 4 - o[1])))
+    detours = {(2, 2): (3, 3), (3, 2): (0, 3), (2, 3): (3, 0)}
+    offsets = list(detours) + [o for o in offsets if o not in detours]
+
+    def first_leg(index):
+        vy, vz = detours[offsets[index]]
+        return pltpu.make_async_remote_copy(
+            src_ref=columns(*offsets[index]),
+            dst_ref=relay.at[index],
+            send_sem=in_send.at[index],
+            recv_sem=relay_recv.at[index],
+            device_id=device(x, mod(y + vy, 4), mod(z + vz, 4), core),
+            device_id_type=MESH,
+        )
+
+    def second_leg(index):
+        dy, dz = offsets[index]
+        vy, vz = detours[offsets[index]]
+        y_from, z_from = mod(y + 4 - vy, 4), mod(z + 4 - vz, 4)
+        source = device(x, y_from, z_from, core)["gr"]
+        return pltpu.make_async_remote_copy(
+            src_ref=relay.at[index],
+            dst_ref=received.at[source],
+            send_sem=relay_send.at[index],
+            recv_sem=in_recv.at[source],
+            device_id=device(x, mod(y_from + dy, 4), mod(z_from + dz, 4), mod(y_from, 2)),
+            device_id_type=MESH,
+        )
+
     for index, (dy, dz) in enumerate(offsets):
-        if dy or dz:
+        if (dy, dz) in detours:
+            first_leg(index).start()
+        elif dy or dz:
             outward(index, dy, dz).start()
         else:
             @pl.when(at_home)
@@ -175,6 +205,9 @@
             @pl.when(jnp.logical_not(at_home))
             def _():
                 outward(index, 0, 0).start()
+    for index in range(len(detours)):
+        first_leg(index).wait_recv()
+        second_leg(index).start()
     for g in range(16):
         pltpu.make_async_copy(received.at[g], received.at[g], in_recv.at[g]).wait()
         wide[g * CAP:(g + 1) * CAP] = received[g].astype(f32)
@@ -267,7 +300,10 @@
     gram_piece[CAP:2 * CAP] = part[y, z, 1] + small_recv[1, 0] + small_recv[1, 1]
     courier.drain()
     for index, (dy, dz) in enumerate(offsets):
-        if dy or dz:
+        if (dy, dz) in detours:
+            first_leg(index).wait_send()
+            second_leg(index).wait_send()
+        elif dy or dz:
             outward(index, dy, dz).wait_send()
         else:
             @pl.when(jnp.logical_not(at_home))
@@ -282,7 +318,8 @@
 
 def update_kernel(
     slot_rows, gram_piece, panel, result, gram_cols, gram_rows, square, poly,
-    pick, outgoing, send_sem, recv_sem, out_send, out_recv,
+    pick, outgoing, relay, send_sem, recv_sem, out_send, out_recv,
+    relay_recv, relay_send,
 ):
     x, y, z, core = position()
     greet(x, y, z, core)
@@ -390,12 +427,14 @@
     block = y * 4 + z
     at_home = core == mod(y, 2)
     own = panel.at[x, pl.ds(pl.multiple_of(core * RB, RB), RB)]
-    chunks = ((0, 512), (512, 640))
+    chunks = ((0, 256), (256, 384), (640, 512))
     offsets = [(dh, dz, dc) for dh in (1, 0) for dz in (2, 1, 3, 0) for dc in (1, 0)]
-
-    def place(dh, dz, dc):
-        y_to = core + 2 * mod(lax.div(y, jnp.int32(2)) + dh, 2)
-        z_to, core_to = mod(z + dz, 4), mod(core + dc, 2)
+    detours = [(1, 2, 1), (0, 2, 1), (1, 1, 1), (1, 3, 1), (1, 0, 1)]
+    offsets = detours + [o for o in offsets if o not in detours]
+
+    def place(dh, dz, dc, y_from=y, z_from=z):
+        y_to = core + 2 * mod(lax.div(y_from, jnp.int32(2)) + dh, 2)
+        z_to, core_to = mod(z_from + dz, 4), mod(core + dc, 2)
         return y_to, z_to, core_to
 
     def window(source, low, size):
@@ -412,6 +451,54 @@
             device_id=device(x, y_to, z_to, core_to),
             device_id_type=MESH,
         )
+
+    def relay_at(index):
+        side = 1 + 2 * core
+        if index == 0:
+            return (
+                mod(y + jnp.where(at_home, 3, side), 4), mod(z + 3, 4),
+                mod(y + jnp.where(at_home, 4 - side, 1), 4), mod(z + 1, 4),
+            )
+        if index == 1:
+            return y, mod(z + 3, 4), y, mod(z + 1, 4)
+        return mod(y + 3, 4), z, mod(y + 1, 4), z
+
+    def first_leg(chunk, index):
+        low, size = chunks[chunk]
+        y_to, z_to, _, _ = relay_at(index)
+        return pltpu.make_async_remote_copy(
+            src_ref=outgoing.at[index, :, low:low + size],
+            dst_ref=relay.at[index, :, low:low + size],
+            send_sem=out_send.at[chunk, index],
+            recv_sem=relay_recv.at[chunk, index],
+            device_id=device(x, y_to, z_to, core),
+            device_id_type=MESH,
+        )
+
+    def second_leg(chunk, index):
+        low, size = chunks[chunk]
+        _, _, y_from, z_from = relay_at(index)
+        y_to, z_to, core_to = place(*offsets[index], y_from, z_from)
+        source = y_from * 4 + z_from
+        return pltpu.make_async_remote_copy(
+            src_ref=relay.at[index, :, low:low + size],
+            dst_ref=window(source, low, size),
+            send_sem=relay_send.at[chunk, index],
+            recv_sem=out_recv.at[chunk, source],
+            device_id=device(x, y_to, z_to, core_to),
+            device_id_type=MESH,
+        )
+
+    def pass_on(chunk):
+        for index in range(len(detours)):
+            if index < 2:
+                first_leg(chunk, index).wait_recv()
+                second_leg(chunk, index).start()
+            else:
+                @pl.when(jnp.logical_not(at_home))
+                def _():
+                    first_leg(chunk, index).wait_recv()
+                    second_leg(chunk, index).start()
 
     row_ids = lax.broadcasted_iota(jnp.int32, (CAP, RB), 1)
     for index, offset in enumerate(offsets):
@@ -432,7 +519,17 @@
         moved = moved + jnp.dot(pick[...].astype(bf16), rest, preferred_element_type=f32)
         outgoing[:, :, low:low + size] = moved.reshape(16, CAP, size)
         for index, offset in enumerate(offsets):
-            if any(offset):
+            if index < 2:
+                first_leg(chunk, index).start()
+            elif index < len(detours):
+                @pl.when(at_home)
+                def _():
+                    first_leg(chunk, index).start()
+
+                @pl.when(jnp.logical_not(at_home))
+                def _():
+                    outward(chunk, index, offset).start()
+            elif any(offset):
                 outward(chunk, index, offset).start()
             else:
                 @pl.when(at_home)
@@ -445,6 +542,9 @@
                 @pl.when(jnp.logical_not(at_home))
                 def _():
                     outward(chunk, index, offset).start()
+        if chunk:
+            pass_on(chunk - 1)
+    pass_on(len(chunks) - 1)
     for chunk, (low, size) in enumerate(chunks):
         for source in range(16):
             pltpu.make_async_copy(
@@ -453,7 +553,19 @@
     courier.drain()
     for chunk in range(len(chunks)):
         for index, offset in enumerate(offsets):
-            if any(offset):
+            if index < 2:
+                first_leg(chunk, index).wait_send()
+                second_leg(chunk, index).wait_send()
+            elif index < len(detours):
+                @pl.when(at_home)
+                def _():
+                    first_leg(chunk, index).wait_send()
+
+                @pl.when(jnp.logical_not(at_home))
+                def _():
+                    outward(chunk, index, offset).wait_send()
+                    second_leg(chunk, index).wait_send()
+            elif any(offset):
                 outward(chunk, index, offset).wait_send()
             else:
                 @pl.when(jnp.logical_not(at_home))
@@ -494,10 +606,13 @@
             pltpu.VMEM((2, 32, PIECE_COLS), f32),
             pltpu.VMEM((2, CAP - 32, PIECE_COLS), f32),
             pltpu.VMEM((2, 2, CAP, PIECE_COLS), f32),
+            pltpu.VMEM((3, CAP, WIDTH), bf16),
             pltpu.SemaphoreType.DMA((40,)),
             pltpu.SemaphoreType.DMA((40,)),
             pltpu.SemaphoreType.DMA((16,)),
             pltpu.SemaphoreType.DMA((16,)),
+            pltpu.SemaphoreType.DMA((3,)),
+            pltpu.SemaphoreType.DMA((3,)),
         ],
         compiler_params=pltpu.CompilerParams(
             collective_id=0, has_side_effects=True, vmem_limit_bytes=VMEM_LIMIT
@@ -517,10 +632,13 @@
             pltpu.VMEM((2, 4, 4, PIECE_ROWS, PIECE_COLS), bf16),
             pltpu.VMEM((16 * CAP, RB), f32),
             pltpu.VMEM((16, CAP, WIDTH), f32),
+            pltpu.VMEM((5, CAP, WIDTH), f32),
             pltpu.SemaphoreType.DMA((64,)),
             pltpu.SemaphoreType.DMA((64,)),
-            pltpu.SemaphoreType.DMA((2, 16)),
-            pltpu.SemaphoreType.DMA((2, 16)),
+            pltpu.SemaphoreType.DMA((3, 16)),
+            pltpu.SemaphoreType.DMA((3, 16)),
+            pltpu.SemaphoreType.DMA((3, 5)),
+            pltpu.SemaphoreType.DMA((3, 5)),
         ],
         compiler_params=pltpu.CompilerParams(
             collective_id=1, has_side_effects=True, vmem_limit_bytes=VMEM_LIMIT

time: 280 us -> 283 us (1.011); the launches traced: 275 us -> 283 us
  Pallas kernels: 267 us -> 274 us
    pallas_call x1, Pallas kernels: 147 us -> 154 us  [body(): pl.pallas_call(update_kernel, name='update_kernel', out_shape=jax.ShapeDt...]
where the time goes in v2:
time: 283 us
  Pallas kernels  274 us (97%)
  local copies, waits for them, and re-layouts  6.49 us (2%)
    pallas_call x1, Pallas kernels, body(): pl.pallas_call(update_kernel, name='update_kernel', out_shape=jax.ShapeDt...  154 us
    pallas_call x1, Pallas kernels, body(): pl.pallas_call(gram_kernel, name='gram_kernel', out_shape=(jax.ShapeDtype...  121 us

profile of v2, /device:TPU:1, one launch (start us, length us, event | category | flops | bytes accessed | tf_op | source)
XLA Modules:
  0.0 282.8 jit_solution(5705790020057238029)
XLA Ops:
  0.0 0.7 fusion
  0.7 0.7 constant_dynamic-slice_fusion
  1.4 0.2 reduce_window_sum.11
  1.6 0.7 subtract_bitcast_fusion
  2.3 0.1 add_select_fusion.1
  2.3 0.7 select_n.29.target_rows
  3.0 1.0 add_select_fusion.slot_rows
  4.0 120.7 %gram_kernel.1 = (bf16[4,896,1152]{2,1,0:T(8,128)(2,1)}, f32[112,896]{1,0:T(8,128)}) custom-call(bf16[56,18432]{1,0:T(8,128)(2,1)} %bitcast.7, s32[1,896]{1,0:T(1,128)} %select_n.29.target_rows), custom_call_target="tpu_custom_call" | custom-call | tf_op jit(solution)/shard_map/gram_kernel/pallas_call | solution.py:591
  124.7 153.6 %update_kernel.1 = f32[56,18432]{1,0:T(8,128)} custom-call(s32[16,56,1]{2,1,0:T(8,128)} %add_select_fusion.slot_rows, f32[112,896]{1,0:T(8,128)} %get-tuple-element.7.gram_piece, bf16[4,896,1152]{2,1,0:T(8,128)(2,1)} %get-tuple-element.8.panel), custom_call_target="tpu_custom_call" | custom-call | tf_op jit(solution)/shard_map/update_kernel/pallas_call | solution.py:622
  278.3 4.4 %copy.4 = f32[1,1,56,18432]{3,2,1,0:T(8,128)} copy(f32[1,1,56,18432]{3,2,1,0:T(8,128)} %bitcast.6) | data formatting | bytes 8257536

commit v3 on v1

--- a/solution.py
+++ b/solution.py
@@ -148,84 +148,120 @@
     me = lax.axis_index("gr")
     at_home = core == y_lo
 
-    def columns(dy, dz):
+    chunks = ((0, 512), (512, 640))
+
+    def columns(chunk, dy, dz):
+        low, size = chunks[chunk]
         block = mod(y + dy, 4) * 4 + mod(z + dz, 4)
-        return shard.at[:, pl.ds(pl.multiple_of(block * WIDTH, 128), WIDTH)]
-
-    def outward(index, dy, dz):
+        return shard.at[:, pl.ds(pl.multiple_of(block * WIDTH + low, 128), size)]
+
+    def landing(chunk, source):
+        low, size = chunks[chunk]
+        return received.at[source, :, low:low + size]
+
+    def outward(chunk, index, dy, dz):
         return pltpu.make_async_remote_copy(
-            src_ref=columns(dy, dz),
-            dst_ref=received.at[me],
-            send_sem=in_send.at[index],
-            recv_sem=in_recv.at[me],
+            src_ref=columns(chunk, dy, dz),
+            dst_ref=landing(chunk, me),
+            send_sem=in_send.at[chunk, index],
+            recv_sem=in_recv.at[chunk, me],
             device_id=device(x, mod(y + dy, 4), mod(z + dz, 4), y_lo),
             device_id_type=MESH,
         )
 
     offsets = [(dy, dz) for dy in range(4) for dz in range(4)]
     offsets = sorted(offsets, key=lambda o: -(min(o[0], 4 - o[0]) + min(o[1], 4 - o[1])))
-    for index, (dy, dz) in enumerate(offsets):
-        if dy or dz:
-            outward(index, dy, dz).start()
-        else:
-            @pl.when(at_home)
-            def _():
-                pltpu.make_async_copy(columns(0, 0), received.at[me], in_recv.at[me]).start()
-
-            @pl.when(jnp.logical_not(at_home))
-            def _():
-                outward(index, 0, 0).start()
-    for g in range(16):
-        pltpu.make_async_copy(received.at[g], received.at[g], in_recv.at[g]).wait()
-        wide[g * CAP:(g + 1) * CAP] = received[g].astype(f32)
-
+    for chunk in range(2):
+        for index, (dy, dz) in enumerate(offsets):
+            if dy or dz:
+                outward(chunk, index, dy, dz).start()
+            else:
+                @pl.when(at_home)
+                def _():
+                    pltpu.make_async_copy(
+                        columns(chunk, 0, 0), landing(chunk, me), in_recv.at[chunk, me]
+                    ).start()
+
+                @pl.when(jnp.logical_not(at_home))
+                def _():
+                    outward(chunk, index, 0, 0).start()
+
+    courier = Courier(send_sem, recv_sem)
+    partner = device(x, y, z, 1 - core)
+    x_right, x_left = device(mod(x + 1, 4), y, z, core), device(mod(x + 3, 4), y, z, core)
     rows = lax.broadcasted_iota(jnp.int32, (RB, 16 * CAP), 0)
-    pick = (rows == target_rows[...]).astype(f32).astype(bf16)
     own = panel.at[x, pl.ds(pl.multiple_of(core * RB, RB), RB)]
-    for low, size in ((0, 512), (512, 640)):
+    across = [[], []]
+
+    def assemble(chunk):
+        low, size = chunks[chunk]
+        for g in range(16):
+            pltpu.make_async_copy(
+                landing(chunk, g), landing(chunk, g), in_recv.at[chunk, g]
+            ).wait()
+            wide[g * CAP:(g + 1) * CAP, low:low + size] = (
+                received[g, :, low:low + size].astype(f32)
+            )
+        pick = (rows == target_rows[...]).astype(f32).astype(bf16)
         own[:, low:low + size] = jnp.dot(
             pick, wide[:, low:low + size].astype(bf16), preferred_element_type=f32
         ).astype(bf16)
 
-    courier = Courier(send_sem, recv_sem)
-    partner = device(x, y, z, 1 - core)
-
-    def slot(low):
+    def rows_of(chunk, first, count):
+        low, size = chunks[chunk]
+
         def part_of(pos):
-            return panel.at[pos, pl.ds(pl.multiple_of(core * RB + low, 32), RB // 2)]
+            start = pl.multiple_of(core * RB + first, 32)
+            return panel.at[pos, pl.ds(start, count), low:low + size]
         return part_of
 
-    def whole(pos):
-        return panel.at[pos, pl.ds(pl.multiple_of(core * RB, 32), RB)]
-
-    ring = RingGather(
-        courier, slot(0), slot(RB // 2), x,
-        device(mod(x + 1, 4), y, z, core), device(mod(x + 3, 4), y, z, core),
-    )
-    across = [courier.send(whole(x), whole(x), partner)]
-
-    def multiply(pos):
+    def ring(chunk):
+        return RingGather(
+            courier, rows_of(chunk, 0, RB // 2), rows_of(chunk, RB // 2, RB // 2),
+            x, x_right, x_left,
+        )
+
+    def forward(chunk, pos):
+        ref = rows_of(chunk, 0, RB)(pos)
+        across[chunk].append(courier.send(ref, ref, partner))
+
+    def multiply(chunk, order):
+        low, size = chunks[chunk]
+        pos = mod(x + (0, 1, 3, 2)[order], 4)
+        across[chunk][order].wait_recv()
         product = lax.dot_general(
-            own[...], panel[pos], (((1,), (1,)), ((), ())), preferred_element_type=f32
-        )
-        part[pos] = (product * (1.0 / N)).reshape(4, 2, CAP, PIECE_COLS)
-
-    ring.relay()
-    ring.near()
-    for step in (1, 3):
-        pos = mod(x + step, 4)
-        across.append(courier.send(whole(pos), whole(pos), partner))
-    across[0].wait_recv()
-    multiply(x)
-    across[1].wait_recv()
-    multiply(mod(x + 1, 4))
-    across[2].wait_recv()
-    multiply(mod(x + 3, 4))
-    ring.far()
-    pos = mod(x + 2, 4)
-    across.append(courier.send(whole(pos), whole(pos), partner))
-    across[3].wait_recv()
-    multiply(pos)
+            own[:, low:low + size], panel[pos, :, low:low + size],
+            (((1,), (1,)), ((), ())), preferred_element_type=f32,
+        )
+        product = (product * (1.0 / N)).reshape(4, 2, CAP, PIECE_COLS)
+        part[pos] = part[pos] + product if chunk else product
+
+    assemble(0)
+    ring_0 = ring(0)
+    forward(0, x)
+    ring_0.relay()
+    ring_0.near()
+    forward(0, mod(x + 1, 4))
+    forward(0, mod(x + 3, 4))
+    assemble(1)
+    ring_1 = ring(1)
+    forward(1, x)
+    multiply(0, 0)
+    ring_0.far()
+    forward(0, mod(x + 2, 4))
+    ring_1.relay()
+    multiply(0, 1)
+    multiply(0, 2)
+    multiply(0, 3)
+    ring_1.near()
+    forward(1, mod(x + 1, 4))
+    forward(1, mod(x + 3, 4))
+    multiply(1, 0)
+    multiply(1, 1)
+    multiply(1, 2)
+    ring_1.far()
+    forward(1, mod(x + 2, 4))
+    multiply(1, 3)
 
     z_right, z_left = device(x, y, mod(z + 1, 4), core), device(x, y, mod(z + 3, 4), core)
     y_right, y_left = device(x, mod(y + 1, 4), z, core), device(x, mod(y + 3, 4), z, core)
@@ -266,13 +302,14 @@
     four.finish()
     gram_piece[CAP:2 * CAP] = part[y, z, 1] + small_recv[1, 0] + small_recv[1, 1]
     courier.drain()
-    for index, (dy, dz) in enumerate(offsets):
-        if dy or dz:
-            outward(index, dy, dz).wait_send()
-        else:
-            @pl.when(jnp.logical_not(at_home))
-            def _():
-                outward(index, 0, 0).wait_send()
+    for chunk in range(2):
+        for index, (dy, dz) in enumerate(offsets):
+            if dy or dz:
+                outward(chunk, index, dy, dz).wait_send()
+            else:
+                @pl.when(jnp.logical_not(at_home))
+                def _():
+                    outward(chunk, index, 0, 0).wait_send()
 
 
 def split(value):
@@ -282,7 +319,7 @@
 
 def update_kernel(
     slot_rows, gram_piece, panel, result, gram_cols, gram_rows, square, poly,
-    pick, outgoing, send_sem, recv_sem, out_send, out_recv,
+    pick, sums, outgoing, send_sem, recv_sem, out_send, out_recv,
 ):
     x, y, z, core = position()
     greet(x, y, z, core)
@@ -338,25 +375,30 @@
     lo_z.near()
     for step in (1, 3):
         across.append(forward(gram_cols.at[1, :, core, mod(z + step, 4)]))
+
+    def square_high(m):
+        left = jnp.concatenate([gram_rows[0, m], gram_rows[1, m]], axis=0)
+        both = jnp.dot(
+            left, gram_cols[0, m].reshape(PIECE_COLS, PIECE_COLS), preferred_element_type=f32
+        )
+        return both[0:PIECE_ROWS] + both[PIECE_ROWS:]
+
+    across[0].wait_recv()
+    square[...] = square_high(x)
     hi_x.far()
     across.append(forward(gram_cols.at[0, mod(x + 2, 4), core]))
     lo_z.far()
     across.append(forward(gram_cols.at[1, :, core, mod(z + 2, 4)]))
-    for copy in across:
+    for step, copy in ((1, across[2]), (3, across[3]), (2, across[6])):
         copy.wait_recv()
-
-    square[...] = jnp.zeros_like(square)
+        square[...] += square_high(mod(x + step, 4))
+    for index in (1, 4, 5, 7):
+        across[index].wait_recv()
 
     @pl.loop(0, 4)
     def _(m):
-        high = gram_cols[0, m].reshape(PIECE_COLS, PIECE_COLS)
         low = gram_cols[1, m].reshape(PIECE_COLS, PIECE_COLS)
-        left = jnp.concatenate([gram_rows[0, m], gram_rows[1, m]], axis=0)
-        both = jnp.dot(left, high, preferred_element_type=f32)
-        square[...] += (
-            both[0:PIECE_ROWS] + both[PIECE_ROWS:]
-            + jnp.dot(gram_rows[0, m], low, preferred_element_type=f32)
-        )
+        square[...] += jnp.dot(gram_rows[0, m], low, preferred_element_type=f32)
 
     for h, value in enumerate(split(cubic_coef * gram_piece[...] + quintic_coef * square[...])):
         poly[h, y, z] = value
@@ -368,6 +410,19 @@
         courier, lambda p: upper(poly.at[1, p, z]), lambda p: lower(poly.at[1, p, z]),
         y, y_right, y_left,
     )
+    own = panel.at[x, pl.ds(pl.multiple_of(core * RB, RB), RB)]
+    sums[...] = linear_coef * own[...].astype(f32)
+
+    def term(h, m, low, size):
+        return jnp.dot(
+            poly[h, m].reshape(RB, PIECE_COLS), panel[m, :, low:low + size],
+            preferred_element_type=f32,
+        )
+
+    def add_high(m):
+        for low, size in ((0, 640), (640, 512)):
+            sums[:, low:low + size] += term(0, m, low, size)
+
     hi_z.relay()
     lo_y.relay()
     hi_z.near()
@@ -380,17 +435,19 @@
     lo_z = RingGather(
         courier, lambda p: poly.at[1, 0:2, p], lambda p: poly.at[1, 2:4, p], z, z_right, z_left,
     )
+    add_high(y)
     hi_y.relay()
     lo_z.relay()
     hi_y.near()
+    add_high(mod(y + 1, 4))
+    add_high(mod(y + 3, 4))
     lo_z.near()
     hi_y.far()
     lo_z.far()
 
     block = y * 4 + z
     at_home = core == mod(y, 2)
-    own = panel.at[x, pl.ds(pl.multiple_of(core * RB, RB), RB)]
-    chunks = ((0, 512), (512, 640))
+    chunks = ((0, 256), (256, 384), (640, 512))
     offsets = [(dh, dz, dc) for dh in (1, 0) for dz in (2, 1, 3, 0) for dc in (1, 0)]
 
     def place(dh, dz, dc):
@@ -420,13 +477,9 @@
         pick[index * CAP:(index + 1) * CAP] = (row_ids == slot_rows[g]).astype(f32)
 
     for chunk, (low, size) in enumerate(chunks):
-        total = linear_coef * own[:, low:low + size].astype(f32)
+        total = sums[:, low:low + size] + term(0, mod(y + 2, 4), low, size)
         for m in range(4):
-            for h in range(2):
-                total = total + jnp.dot(
-                    poly[h, m].reshape(RB, PIECE_COLS), panel[m, :, low:low + size],
-                    preferred_element_type=f32,
-                )
+            total = total + term(1, m, low, size)
         high, rest = split(total)
         moved = jnp.dot(pick[...].astype(bf16), high, preferred_element_type=f32)
         moved = moved + jnp.dot(pick[...].astype(bf16), rest, preferred_element_type=f32)
@@ -494,10 +547,10 @@
             pltpu.VMEM((2, 32, PIECE_COLS), f32),
             pltpu.VMEM((2, CAP - 32, PIECE_COLS), f32),
             pltpu.VMEM((2, 2, CAP, PIECE_COLS), f32),
-            pltpu.SemaphoreType.DMA((40,)),
-            pltpu.SemaphoreType.DMA((40,)),
-            pltpu.SemaphoreType.DMA((16,)),
-            pltpu.SemaphoreType.DMA((16,)),
+            pltpu.SemaphoreType.DMA((56,)),
+            pltpu.SemaphoreType.DMA((56,)),
+            pltpu.SemaphoreType.DMA((2, 16)),
+            pltpu.SemaphoreType.DMA((2, 16)),
         ],
         compiler_params=pltpu.CompilerParams(
             collective_id=0, has_side_effects=True, vmem_limit_bytes=VMEM_LIMIT
@@ -516,11 +569,12 @@
             pltpu.VMEM((PIECE_ROWS, PIECE_COLS), f32),
             pltpu.VMEM((2, 4, 4, PIECE_ROWS, PIECE_COLS), bf16),
             pltpu.VMEM((16 * CAP, RB), f32),
+            pltpu.VMEM((RB, WIDTH), f32),
             pltpu.VMEM((16, CAP, WIDTH), f32),
             pltpu.SemaphoreType.DMA((64,)),
             pltpu.SemaphoreType.DMA((64,)),
-            pltpu.SemaphoreType.DMA((2, 16)),
-            pltpu.SemaphoreType.DMA((2, 16)),
+            pltpu.SemaphoreType.DMA((3, 16)),
+            pltpu.SemaphoreType.DMA((3, 16)),
         ],
         compiler_params=pltpu.CompilerParams(
             collective_id=1, has_side_effects=True, vmem_limit_bytes=VMEM_LIMIT

time: 280 us -> 265 us (0.946); the launches traced: 275 us -> 264 us
  Pallas kernels: 267 us -> 255 us
    pallas_call x1, Pallas kernels: 119 us -> 105 us  [body(): pl.pallas_call(gram_kernel, name='gram_kernel', out_shape=(jax.ShapeDtype...]
    pallas_call x1, Pallas kernels: 147 us -> 150 us  [body(): pl.pallas_call(update_kernel, name='update_kernel', out_shape=jax.ShapeDt...]
where the time goes in v3:
time: 265 us; the launch traced here: 264 us
  Pallas kernels  255 us (96%)
  local copies, waits for them, and re-layouts  6.49 us (2%)
    pallas_call x1, Pallas kernels, body(): pl.pallas_call(update_kernel, name='update_kernel', out_shape=jax.ShapeDt...  150 us
    pallas_call x1, Pallas kernels, body(): pl.pallas_call(gram_kernel, name='gram_kernel', out_shape=(jax.ShapeDtype...  105 us

profile of v3, /device:TPU:1, one launch (start us, length us, event | category | flops | bytes accessed | tf_op | source)
XLA Modules:
  0.0 263.6 jit_solution(10261491759932588085)
XLA Ops:
  0.0 0.7 fusion
  0.7 0.7 constant_dynamic-slice_fusion
  1.4 0.2 reduce_window_sum.11
  1.6 0.7 subtract_bitcast_fusion
  2.3 0.1 add_select_fusion.1
  2.3 0.7 select_n.29.target_rows
  3.0 1.0 add_select_fusion.slot_rows
  4.0 105.1 %gram_kernel.1 = (bf16[4,896,1152]{2,1,0:T(8,128)(2,1)}, f32[112,896]{1,0:T(8,128)}) custom-call(bf16[56,18432]{1,0:T(8,128)(2,1)} %bitcast.7, s32[1,896]{1,0:T(1,128)} %select_n.29.target_rows), custom_call_target="tpu_custom_call" | custom-call | tf_op jit(solution)/shard_map/gram_kernel/pallas_call | solution.py:532
  109.1 150.1 %update_kernel.1 = f32[56,18432]{1,0:T(8,128)} custom-call(s32[16,56,1]{2,1,0:T(8,128)} %add_select_fusion.slot_rows, f32[112,896]{1,0:T(8,128)} %get-tuple-element.7.gram_piece, bf16[4,896,1152]{2,1,0:T(8,128)(2,1)} %get-tuple-element.8.panel), custom_call_target="tpu_custom_call" | custom-call | tf_op jit(solution)/shard_map/update_kernel/pallas_call | solution.py:560
  259.1 4.4 %copy.4 = f32[1,1,56,18432]{3,2,1,0:T(8,128)} copy(f32[1,1,56,18432]{3,2,1,0:T(8,128)} %bitcast.6) | data formatting | bytes 8257536

commit v4 on v3

--- a/solution.py
+++ b/solution.py
@@ -116,11 +116,20 @@
         self.pos, self.right, self.left = pos, right, left
         self.tmp_a, self.tmp_b, self.from_left, self.from_right = bufs
         self.in_a, self.in_b = cut
-        far = mod(pos + 2, 4)
-        self.a1 = courier.send(part_a(far), self.tmp_a, right)
-        self.b1 = courier.send(part_b(far), self.tmp_b, left)
-        self.a2 = courier.send(part_b(mod(pos + 1, 4)), self.in_b(self.from_left), right)
-        self.b2 = courier.send(part_a(mod(pos + 3, 4)), self.in_a(self.from_right), left)
+
+    def start_a(self):
+        send, pos, part = self.courier.send, self.pos, self.part_a
+        self.a1 = send(part(mod(pos + 2, 4)), self.tmp_a, self.right)
+        self.b2 = send(part(mod(pos + 3, 4)), self.in_a(self.from_right), self.left)
+
+    def start_b(self):
+        send, pos, part = self.courier.send, self.pos, self.part_b
+        self.b1 = send(part(mod(pos + 2, 4)), self.tmp_b, self.left)
+        self.a2 = send(part(mod(pos + 1, 4)), self.in_b(self.from_left), self.right)
+
+    def start(self):
+        self.start_a()
+        self.start_b()
 
     def relay(self):
         self.a1.wait_recv()
@@ -234,7 +243,7 @@
             (((1,), (1,)), ((), ())), preferred_element_type=f32,
         )
         product = (product * (1.0 / N)).reshape(4, 2, CAP, PIECE_COLS)
-        part[pos] = part[pos] + product if chunk else product
+        part[order] = part[order] + product if chunk else product
 
     assemble(0)
     ring_0 = ring(0)
@@ -256,51 +265,60 @@
     ring_1.near()
     forward(1, mod(x + 1, 4))
     forward(1, mod(x + 3, 4))
+    z_right, z_left = device(x, y, mod(z + 1, 4), core), device(x, y, mod(z + 3, 4), core)
+    y_right, y_left = device(x, mod(y + 1, 4), z, core), device(x, mod(y + 3, 4), z, core)
+    first, second = (lambda r: r.at[0:2]), (lambda r: r.at[2:4])
+    upper, lower = (lambda r: r.at[0:32]), (lambda r: r.at[32:CAP])
+
+    def bufs(tmp_a, tmp_b, recv, half):
+        return tmp_a.at[half], tmp_b.at[half], recv.at[half, 0], recv.at[half, 1]
+
+    big = lambda half: bufs(big_tmp.at[0], big_tmp.at[1], big_recv, half)
+    small = lambda half: bufs(small_tmp_a, small_tmp_b, small_recv, half)
+    def at(p):
+        step = mod(p + 4 - x, 4)
+        return step + lax.div(step, jnp.int32(2)) * (5 - 2 * step)
+
+    one = RingReduce(
+        courier, lambda p: part.at[0:2, p, 0], lambda p: part.at[2:4, p, 0],
+        big(0), (first, second), z, z_right, z_left,
+    )
+    two = RingReduce(
+        courier, lambda p: part.at[at(p), 0:2, 1], lambda p: part.at[at(p), 2:4, 1],
+        big(1), (first, second), y, y_right, y_left,
+    )
     multiply(1, 0)
     multiply(1, 1)
+    one.start_a()
     multiply(1, 2)
     ring_1.far()
     forward(1, mod(x + 2, 4))
     multiply(1, 3)
-
-    z_right, z_left = device(x, y, mod(z + 1, 4), core), device(x, y, mod(z + 3, 4), core)
-    y_right, y_left = device(x, mod(y + 1, 4), z, core), device(x, mod(y + 3, 4), z, core)
-    first, second = (lambda r: r.at[0:2]), (lambda r: r.at[2:4])
-    upper, lower = (lambda r: r.at[0:32]), (lambda r: r.at[32:CAP])
-
-    def bufs(tmp_a, tmp_b, recv, half):
-        return tmp_a.at[half], tmp_b.at[half], recv.at[half, 0], recv.at[half, 1]
-
-    big = lambda half: bufs(big_tmp.at[0], big_tmp.at[1], big_recv, half)
-    small = lambda half: bufs(small_tmp_a, small_tmp_b, small_recv, half)
-    one = RingReduce(
-        courier, lambda p: part.at[0:2, p, 0], lambda p: part.at[2:4, p, 0],
-        big(0), (first, second), z, z_right, z_left,
-    )
-    two = RingReduce(
-        courier, lambda p: part.at[p, 0:2, 1], lambda p: part.at[p, 2:4, 1],
-        big(1), (first, second), y, y_right, y_left,
-    )
+    one.start_b()
+    two.start()
     one.relay()
     two.relay()
     one.finish()
     part[:, z, 0] = part[:, z, 0] + big_recv[0, 0] + big_recv[0, 1]
     three = RingReduce(
-        courier, lambda p: upper(part.at[p, z, 0]), lambda p: lower(part.at[p, z, 0]),
+        courier, lambda p: upper(part.at[at(p), z, 0]), lambda p: lower(part.at[at(p), z, 0]),
         small(0), (upper, lower), y, y_right, y_left,
     )
+    three.start()
     two.finish()
-    part[y, :, 1] = part[y, :, 1] + big_recv[1, 0] + big_recv[1, 1]
+    mine = at(y)
+    part[mine, :, 1] = part[mine, :, 1] + big_recv[1, 0] + big_recv[1, 1]
     four = RingReduce(
-        courier, lambda p: upper(part.at[y, p, 1]), lambda p: lower(part.at[y, p, 1]),
+        courier, lambda p: upper(part.at[mine, p, 1]), lambda p: lower(part.at[mine, p, 1]),
         small(1), (upper, lower), z, z_right, z_left,
     )
+    four.start()
     three.relay()
     four.relay()
     three.finish()
-    gram_piece[0:CAP] = part[y, z, 0] + small_recv[0, 0] + small_recv[0, 1]
+    gram_piece[0:CAP] = part[mine, z, 0] + small_recv[0, 0] + small_recv[0, 1]
     four.finish()
-    gram_piece[CAP:2 * CAP] = part[y, z, 1] + small_recv[1, 0] + small_recv[1, 1]
+    gram_piece[CAP:2 * CAP] = part[mine, z, 1] + small_recv[1, 0] + small_recv[1, 1]
     courier.drain()
     for chunk in range(2):
         for index, (dy, dz) in enumerate(offsets):

time: 265 us -> 266 us (level)
  no operation moved by 1% of the time
where the time goes in v4:
time: 266 us; the launch traced here: 264 us
  Pallas kernels  256 us (96%)
  local copies, waits for them, and re-layouts  6.49 us (2%)
    pallas_call x1, Pallas kernels, body(): pl.pallas_call(update_kernel, name='update_kernel', out_shape=jax.ShapeDt...  151 us
    pallas_call x1, Pallas kernels, body(): pl.pallas_call(gram_kernel, name='gram_kernel', out_shape=(jax.ShapeDtype...  105 us

profile of v4, /device:TPU:1, one launch (start us, length us, event | category | flops | bytes accessed | tf_op | source)
XLA Modules:
  0.0 264.4 jit_solution(10845306232279547277)
XLA Ops:
  0.0 0.7 fusion
  0.7 0.7 constant_dynamic-slice_fusion
  1.4 0.2 reduce_window_sum.11
  1.6 0.7 subtract_bitcast_fusion
  2.3 0.1 add_select_fusion.1
  2.3 0.7 select_n.29.target_rows
  3.0 1.0 add_select_fusion.slot_rows
  4.0 104.7 %gram_kernel.1 = (bf16[4,896,1152]{2,1,0:T(8,128)(2,1)}, f32[112,896]{1,0:T(8,128)}) custom-call(bf16[56,18432]{1,0:T(8,128)(2,1)} %bitcast.7, s32[1,896]{1,0:T(1,128)} %select_n.29.target_rows), custom_call_target="tpu_custom_call" | custom-call | tf_op jit(solution)/shard_map/gram_kernel/pallas_call | solution.py:550
  108.7 151.2 %update_kernel.1 = f32[56,18432]{1,0:T(8,128)} custom-call(s32[16,56,1]{2,1,0:T(8,128)} %add_select_fusion.slot_rows, f32[112,896]{1,0:T(8,128)} %get-tuple-element.7.gram_piece, bf16[4,896,1152]{2,1,0:T(8,128)(2,1)} %get-tuple-element.8.panel), custom_call_target="tpu_custom_call" | custom-call | tf_op jit(solution)/shard_map/update_kernel/pallas_call | solution.py:578
  260.0 4.4 %copy.4 = f32[1,1,56,18432]{3,2,1,0:T(8,128)} copy(f32[1,1,56,18432]{3,2,1,0:T(8,128)} %bitcast.6) | data formatting | bytes 8257536

commit v5 on v3

--- a/solution.py
+++ b/solution.py
@@ -148,7 +148,7 @@
     me = lax.axis_index("gr")
     at_home = core == y_lo
 
-    chunks = ((0, 512), (512, 640))
+    chunks = ((0, 384), (384, 768))
 
     def columns(chunk, dy, dz):
         low, size = chunks[chunk]

time: 265 us -> 262 us (0.989)
  Pallas kernels: 255 us -> 250 us
    pallas_call x1, Pallas kernels: 150 us -> 145 us  [body(): pl.pallas_call(update_kernel, name='update_kernel', out_shape=jax.ShapeDt...]
where the time goes in v5:
time: 262 us; the launch traced here: 259 us
  Pallas kernels  250 us (95%)
  local copies, waits for them, and re-layouts  6.49 us (2%)
    pallas_call x1, Pallas kernels, body(): pl.pallas_call(update_kernel, name='update_kernel', out_shape=jax.ShapeDt...  145 us
    pallas_call x1, Pallas kernels, body(): pl.pallas_call(gram_kernel, name='gram_kernel', out_shape=(jax.ShapeDtype...  105 us

profile of v5, /device:TPU:1, one launch (start us, length us, event | category | flops | bytes accessed | tf_op | source)
XLA Modules:
  0.0 258.9 jit_solution(16357924920841922041)
XLA Ops:
  0.0 0.7 fusion
  0.7 0.7 constant_dynamic-slice_fusion
  1.4 0.2 reduce_window_sum.11
  1.6 0.7 subtract_bitcast_fusion
  2.3 0.1 add_select_fusion.1
  2.3 0.7 select_n.29.target_rows
  3.0 1.0 add_select_fusion.slot_rows
  4.0 105.1 %gram_kernel.1 = (bf16[4,896,1152]{2,1,0:T(8,128)(2,1)}, f32[112,896]{1,0:T(8,128)}) custom-call(bf16[56,18432]{1,0:T(8,128)(2,1)} %bitcast.7, s32[1,896]{1,0:T(1,128)} %select_n.29.target_rows), custom_call_target="tpu_custom_call" | custom-call | tf_op jit(solution)/shard_map/gram_kernel/pallas_call | solution.py:532
  109.1 145.3 %update_kernel.1 = f32[56,18432]{1,0:T(8,128)} custom-call(s32[16,56,1]{2,1,0:T(8,128)} %add_select_fusion.slot_rows, f32[112,896]{1,0:T(8,128)} %get-tuple-element.7.gram_piece, bf16[4,896,1152]{2,1,0:T(8,128)(2,1)} %get-tuple-element.8.panel), custom_call_target="tpu_custom_call" | custom-call | tf_op jit(solution)/shard_map/update_kernel/pallas_call | solution.py:560
  254.5 4.4 %copy.4 = f32[1,1,56,18432]{3,2,1,0:T(8,128)} copy(f32[1,1,56,18432]{3,2,1,0:T(8,128)} %bitcast.6) | data formatting | bytes 8257536
